TPU v7x, 32 devices: a whole 2x2x4 slice. The times are simulated.
32 devices in a mesh: fsdp: 8 (over z, x), tp: 4 (over y, core).
Axes of the slice: x: 2, y: 2, z: 4, core: 2. Of those that a mesh axis runs over, the one named last changes fastest.
Arguments:
- step_input: bfloat16 [4, 768, 8192], P(None, 'fsdp'), may hold values from -6 to 6
- lengths: int32 [768], P('fsdp'), may hold values from 1 to 128, as said below
- cache_k: bfloat16 [768, 128, 1024], P('fsdp', None, 'tp'), may hold values from -500 to 500
- cache_v: bfloat16 [768, 128, 1024], P('fsdp', None, 'tp'), may hold values from -6 to 6
- w_query: bfloat16 [8192, 4096], P('fsdp', 'tp'), may hold values from -0.0625 to 0.0625
- w_key: bfloat16 [8192, 1024], P('fsdp', 'tp'), may hold values from -0.0625 to 0.0625
- w_value: bfloat16 [8192, 1024], P('fsdp', 'tp'), may hold values from -0.0625 to 0.0625
- w_output: bfloat16 [4096, 8192], P('fsdp', 'tp'), may hold values from -0.09375 to 0.09375
- loss_grad: bfloat16 [4, 768, 8192], P(None, 'fsdp', 'tp'), may hold values from -6 to 6
Outputs:
- layer_out: bfloat16 [4, 768, 8192], P(None, 'fsdp', 'tp')
- grad_output: float32 [4096, 8192], P('fsdp', 'tp')
Inputs may be any that keep to these rules, and one draw needn't show every extreme that they name: `lengths`: every row has at least one filled position; some row in every draw is full (128).
All inputs are finite; a program needn't handle non-finite values.
Results may differ from a plain program's by a relative error of at most 0.008.
The roundings to bfloat16 on the way count: a program that leaves them out, or rounds other values in their place, can miss the bound.
Values may be sent and summed in bfloat16 or wider, within the bound.
A program may use at most 128 MiB of HBM per device.

v0:
```python
import jax
import jax.numpy as jnp
from jax import lax
from jax.sharding import PartitionSpec as P

HD = 128


rope_base = 1000000.0


def rotate(vec, pos):
    half = vec.shape[-1] // 2
    freq = rope_base ** (-(jnp.arange(half).astype(jnp.float32) * 2.0) / vec.shape[-1])
    angle = pos[..., None] * freq
    cosine = jnp.cos(angle)
    sine = jnp.sin(angle)
    first = vec[..., :half]
    second = vec[..., half:]
    return jnp.concatenate(
        [first * cosine - second * sine, second * cosine + first * sine], axis=-1
    )


def attend(q_rot, k_new, v_new, cache_k, cache_v, lengths, kv_local, group):
    steps, rows = (q_rot.shape[0], q_rot.shape[1])
    head_size = q_rot.shape[-1]
    cache_len = cache_k.shape[1]
    qg = q_rot.reshape(steps, rows, kv_local, group, head_size)
    kc = cache_k.reshape(rows, cache_len, kv_local, head_size)
    vc = cache_v.reshape(rows, cache_len, kv_local, head_size)
    scale = 1.0 / head_size**0.5
    s_cache = jnp.einsum("srhgd,rchd->srhgc", qg, kc, preferred_element_type=jnp.float32) * scale
    s_new = jnp.einsum("srhgd,trhd->srhgt", qg, k_new, preferred_element_type=jnp.float32) * scale
    valid = (jnp.arange(cache_len)[None, :] < lengths[:, None])[None, :, None, None, :]
    causal = (jnp.arange(steps)[None, :] <= jnp.arange(steps)[:, None])[:, None, None, None, :]
    s_cache = jnp.where(valid, s_cache, -1e30)
    s_new = jnp.where(causal, s_new, -1e30)
    top = jnp.maximum(jnp.max(s_cache, axis=-1), jnp.max(s_new, axis=-1))[..., None]
    e_cache = jnp.where(valid, jnp.exp(s_cache - top), 0.0)
    e_new = jnp.where(causal, jnp.exp(s_new - top), 0.0)
    total = jnp.sum(e_cache, axis=-1, keepdims=True) + jnp.sum(e_new, axis=-1, keepdims=True)
    p_cache = (e_cache / total).astype(jnp.bfloat16)
    p_new = (e_new / total).astype(jnp.bfloat16)
    out = jnp.einsum("srhgc,rchd->srhgd", p_cache, vc, preferred_element_type=jnp.float32)
    out = out + jnp.einsum("srhgt,trhd->srhgd", p_new, v_new, preferred_element_type=jnp.float32)
    return out.astype(jnp.bfloat16).reshape(steps * rows, kv_local * group * head_size)


def shards(step_input, lengths, cache_k, cache_v, w_query, w_key, w_value, w_output, loss_grad):
    steps, rows, width = step_input.shape
    flat = step_input.reshape(steps * rows, width)
    head_size = HD
    kv_local = w_key.shape[1] // head_size
    q_local = w_query.shape[1] // head_size
    group = q_local // kv_local
    out_whole = lax.all_gather(w_output, "fsdp", axis=0, tiled=True)
    q_full, k_full, v_full = (
        lax.all_gather(w_query, "fsdp", axis=0, tiled=True),
        lax.all_gather(w_key, "fsdp", axis=0, tiled=True),
        lax.all_gather(w_value, "fsdp", axis=0, tiled=True),
    )
    query = jnp.dot(flat, q_full, preferred_element_type=jnp.float32)
    key = jnp.dot(flat, k_full, preferred_element_type=jnp.float32)
    value = jnp.dot(flat, v_full, preferred_element_type=jnp.float32)
    pos = lengths.astype(jnp.float32)[None, :] + jnp.arange(steps).astype(jnp.float32)[:, None]
    q_rot = rotate(query.reshape(steps, rows, q_local, head_size), pos[:, :, None]).astype(
        jnp.bfloat16
    )
    k_new = rotate(key.reshape(steps, rows, kv_local, head_size), pos[:, :, None]).astype(
        jnp.bfloat16
    )
    v_new = value.reshape(steps, rows, kv_local, head_size).astype(jnp.bfloat16)
    local_attended = attend(q_rot, k_new, v_new, cache_k, cache_v, lengths, kv_local, group)
    attended = lax.all_gather(local_attended, "tp", axis=1, tiled=True)
    projected = jnp.dot(attended, out_whole, preferred_element_type=jnp.float32)
    layer_out = projected.astype(jnp.bfloat16).reshape(steps, rows, w_output.shape[1])
    upstream = loss_grad.reshape(steps * rows, loss_grad.shape[2])
    grad_output = lax.psum_scatter(
        lax.dot_general(
            attended, upstream, (((0,), (0,)), ((), ())), preferred_element_type=jnp.float32
        ),
        "fsdp",
        scatter_dimension=0,
        tiled=True,
    )
    return (layer_out, grad_output)


def solution(mesh):
    in_specs = (
        P(None, "fsdp", None),
        P("fsdp"),
        P("fsdp", None, "tp"),
        P("fsdp", None, "tp"),
        P("fsdp", "tp"),
        P("fsdp", "tp"),
        P("fsdp", "tp"),
        P("fsdp", "tp"),
        P(None, "fsdp", "tp"),
    )
    out_specs = (P(None, "fsdp", "tp"), P("fsdp", "tp"))
    return jax.shard_map(shards, mesh=mesh, in_specs=in_specs, out_specs=out_specs, check_vma=False)
```

profile of v0, /device:TPU:0, one launch (start us, length us, event | category | flops | bytes accessed | tf_op | source)
XLA Modules:
  0.0 1269.4 jit_solution(3669175318783354331)
XLA Ops:
  8.0 0.7 all-gather.10.cloned.1.call-update
  9.5 9.7 reshape.125
  19.2 9.8 reshape.126
  29.2 0.8 multiply_cosine_fusion
  30.0 56.3 %all-gather.8.cloned.1.call-done = bf16[8192,256]{1,0:T(8,128)(2,1)} async-done(((bf16[1024,256]{1,0:T(8,128)(2,1)}), bf16[8192,256]{1,0:T(8,128)(2,1)}) %all-gather.8.cloned.1.call-update) | async-done | bytes 4194320 | tf_op jit(solution)/shard_map/all_gather | solution.py:60
  86.3 6.3 copy.60
  92.6 67.5 %all-gather.10.cloned.1.call-done = bf16[8192,256]{1,0:T(8,128)(2,1)} async-done(((bf16[1024,256]{1,0:T(8,128)(2,1)}), bf16[8192,256]{1,0:T(8,128)(2,1)}) %all-gather.10.cloned.1.call-update) | async-done | bytes 4194320 | tf_op jit(solution)/shard_map/all_gather | solution.py:61
  160.1 6.4 copy.67
  166.5 7.7 fusion.4
  175.8 2.5 fusion.18
  178.3 209.9 %all-gather.6.cloned.1.call-done = bf16[8192,1024]{1,0:T(8,128)(2,1)} async-done(((bf16[1024,1024]{1,0:T(8,128)(2,1)}), bf16[8192,1024]{1,0:T(8,128)(2,1)}) %all-gather.6.cloned.1.call-update) | async-done | bytes 16777232 | tf_op jit(solution)/shard_map/all_gather | solution.py:59
  388.1 21.0 %copy.56 = bf16[1024,8192]{1,0:T(8,128)(2,1)} copy(bf16[1024,8192]{0,1:T(8,128)(2,1)} %bitcast.72) | data formatting | bytes 33554432 | tf_op jit(solution)/shard_map/dot_general | solution.py:63
  409.1 11.3 fusion.6
  422.3 0.9 copy-done.3
  423.2 7.1 fusion.27
  430.3 0.9 copy.62
  431.4 0.9 copy.63
  432.3 7.5 bitcast_reduce_fusion
  440.1 1.6 fusion.30
  441.7 1.7 copy.65
  443.4 2.7 fusion.21
  446.1 0.8 add.41
  446.9 1.8 copy.68
  448.7 1.5 divide_convert_fusion.2
  450.2 2.2 copy.70
  452.4 5.5 fusion
  459.0 1.4 reshape.127
  461.1 26.2 %all-gather.12.cloned.1.call-done = bf16[384,4096]{1,0:T(8,128)(2,1)} async-done(((bf16[384,1024]{1,0:T(8,128)(2,1)}), bf16[384,4096]{1,0:T(8,128)(2,1)}) %all-gather.12.cloned.1.call-update) | async-done | bytes 3145744 | tf_op jit(solution)/shard_map/all_gather | solution.py:75
  487.3 19.2 %fusion.32 = f32[4096,2048]{1,0:T(8,128)} fusion(bf16[384,4096]{1,0:T(8,128)(2,1)} %all-gather.12.cloned.1.call-done, bf16[384,2048]{1,0:T(8,128)(2,1)S(1)} %bitcast.71), kind=kOutput, calls=%fused_computation.48 | convolution fusion | flops 6442450944 | bytes 38273024 | tf_op jit(solution)/shard_map/dot_general | solution.py:80
  506.5 210.4 %all-gather.14.cloned.1.call-done = bf16[4096,2048]{1,0:T(8,128)(2,1)} async-done(((bf16[512,2048]{1,0:T(8,128)(2,1)}), bf16[4096,2048]{1,0:T(8,128)(2,1)}) %all-gather.14.cloned.1.call-update) | async-done | bytes 16777232 | tf_op jit(solution)/shard_map/all_gather | solution.py:57
  716.9 12.0 convolution_convert_fusion
  728.9 533.6 %reduce-scatter.2.cloned.1.call-done = f32[512,2048]{1,0:T(8,128)} async-done(((f32[4096,2048]{1,0:T(8,128)}), f32[512,2048]{1,0:T(8,128)}) %reduce-scatter.2.cloned.1.call-update) | async-done | bytes 4194320 | tf_op jit(solution)/shard_map/reduce_scatter | solution.py:79
  (55 shorter events, 7.2 us)
Async XLA Ops:
  7.2 480.2 %copy-start = (bf16[4,96,2048]{2,1,0:T(8,128)(2,1)S(1)}, bf16[4,96,2048]{2,1,0:T(8,128)(2,1)}, u32[]{:S(2)}) copy-start(bf16[4,96,2048]{2,1,0:T(8,128)(2,1)} %param.17) | copy-start | bytes 4718596
  7.2 2.3 copy-start.10
  7.2 79.1 %all-gather.8.cloned.1.call-start = ((), (), s32[]{:S(2)}) async-start(), calls=%async_computation.2 | async-start | bytes 4718592 | tf_op jit(solution)/shard_map/all_gather | solution.py:60
  7.9 152.2 %all-gather.10.cloned.1.call-start = ((), (), s32[]{:S(2)}) async-start(), calls=%async_computation.3 | async-start | bytes 4718592 | tf_op jit(solution)/shard_map/all_gather | solution.py:61
  8.7 379.5 %all-gather.6.cloned.1.call-start = ((), (), s32[]{:S(2)}) async-start(), calls=%async_computation.1 | async-start | bytes 18874368 | tf_op jit(solution)/shard_map/all_gather | solution.py:59
  9.4 477.9 %all-gather.12.cloned.1.call-start = ((), (), s32[]{:S(2)}) async-start(), calls=%async_computation.4 | async-start | bytes 3932160 | tf_op jit(solution)/shard_map/all_gather | solution.py:75
  29.0 402.2 %copy-start.9 = (pred[4,4]{1,0:T(4,128)(4,1)}, pred[4,4]{1,0:T(4,128)(4,1)S(1)}, u32[]{:S(2)}) copy-start(pred[4,4]{1,0:T(4,128)(4,1)S(1)} %iota_compare_fusion.1) | copy-start | bytes 52
  29.2 403.1 %copy-start.8 = (pred[96,128]{1,0:T(8,128)(4,1)}, pred[96,128]{1,0:T(8,128)(4,1)S(1)}, u32[]{:S(2)}) copy-start(pred[96,128]{1,0:T(8,128)(4,1)S(1)} %iota_compare_fusion) | copy-start | bytes 36868
  166.5 8.6 slice-start
  166.5 8.6 copy-start.1
  166.5 9.3 slice-start.1
  421.4 0.9 copy-start.2
  422.3 0.9 copy-start.3
  431.2 1.1 copy-start.6
  432.3 7.5 copy-start.4
  443.4 2.7 copy-start.5
  452.4 5.5 copy-start.7
  452.4 5.6 copy-start.11
  460.4 256.5 %all-gather.14.cloned.1.call-start = ((), (), s32[]{:S(2)}) async-start(), calls=%async_computation.5 | async-start | bytes 18874368 | tf_op jit(solution)/shard_map/all_gather | solution.py:57
  461.0 801.5 %reduce-scatter.2.cloned.1.call-start = ((), (), s32[]{:S(2)}) async-start(), calls=%async_computation.6 | async-start | bytes 37748736 | tf_op jit(solution)/shard_map/reduce_scatter | solution.py:79
Sparse Core Ops, SparseCore 0:
  10.1 76.0 all-gather.7
  88.4 71.6 all-gather.9
  162.2 225.8 all-gather.5
  460.6 26.7 all-gather.11
  489.3 227.5 all-gather.13
  721.1 541.3 reduce-scatter.1
where the time goes:
time: 1270 us
  waiting for transfers between devices  1110 us (87%)
  matrix products  73.4 us (6%)
  local copies, waits for them, and re-layouts  66.1 us (5%)
  between operations  14.4 us (1%)
    reduce_scatter x1, waiting for transfers between devices, shards(): lax.psum_scatter(lax.dot_general(attended, upstream, (((0,), (0,)), ((),...  534 us
    all_gather x1, waiting for transfers between devices, shards(): out_whole = lax.all_gather(w_output, 'fsdp', axis=0, tiled=True)  210 us
    all_gather x1, waiting for transfers between devices, shards(): lax.all_gather(w_query, 'fsdp', axis=0, tiled=True)  210 us
    all_gather x1, waiting for transfers between devices, shards(): lax.all_gather(w_value, 'fsdp', axis=0, tiled=True)  67.5 us
    all_gather x1, waiting for transfers between devices, shards(): lax.all_gather(w_key, 'fsdp', axis=0, tiled=True)  56.3 us
    all_gather x1, waiting for transfers between devices, shards(): attended = lax.all_gather(local_attended, 'tp', axis=1, tiled=True)  26.2 us
  transfers between devices with their start and end apart: 6, of which 6 were waited for; matrix products, arithmetic and copies ran while one was open for 6% of the time, Pallas kernels for 0%

commit v1 on v0

--- a/solution.py
+++ b/solution.py
@@ -1,6 +1,10 @@
+import functools
+
 import jax
 import jax.numpy as jnp
 from jax import lax
+from jax.experimental import pallas as pl
+from jax.experimental.pallas import tpu as pltpu
 from jax.sharding import PartitionSpec as P
 
 HD = 128
@@ -47,22 +51,263 @@
     return out.astype(jnp.bfloat16).reshape(steps * rows, kv_local * group * head_size)
 
 
-def shards(step_input, lengths, cache_k, cache_v, w_query, w_key, w_value, w_output, loss_grad):
+def ring_device(place, n):
+    place = place % n
+    back = place // (n // 2)
+    return (1 - back) * (2 * place) + back * (2 * (n - 1 - place) + 1)
+
+
+def ring_place(device, n):
+    odd = device % 2
+    return (1 - odd) * (device // 2) + odd * (n - 1 - device // 2)
+
+
+def remote(src, dst, send, recv, target):
+    return pltpu.make_async_remote_copy(
+        src_ref=src,
+        dst_ref=dst,
+        send_sem=send,
+        recv_sem=recv,
+        device_id=target,
+        device_id_type=pl.DeviceIdType.MESH,
+    )
+
+
+class Ring:
+    def __init__(self, n, cuts, x_ref, o_ref, sems):
+        self.n, self.cuts, self.x_ref, self.o_ref = n, cuts, x_ref, o_ref
+        self.local_sem, self.send_sem, self.recv_sem = sems
+        self.me = lax.axis_index("fsdp")
+        self.place = ring_place(self.me, n)
+        self.ways = (
+            ring_device(self.place + 1, n),
+            ring_device(self.place + n - 1, n),
+        )
+        self.rows = x_ref.shape[0] // (2 * cuts)
+
+    def own(self):
+        return pltpu.make_async_copy(self.x_ref, self.o_ref.at[self.me], self.local_sem)
+
+    def hop(self, step, cut, way):
+        origin = ring_device(self.place + self.n + (step if way else -step), self.n)
+        span = pl.ds((way * self.cuts + cut) * self.rows, self.rows)
+        land = self.o_ref.at[origin, span]
+        return remote(
+            self.x_ref.at[span] if step == 0 else land,
+            land,
+            self.send_sem.at[way, step, cut],
+            self.recv_sem.at[way, step, cut],
+            {"fsdp": self.ways[way]},
+        )
+
+    def arrival(self, step, cut, way):
+        ahead = step + 1 if way else -step - 1
+        origin = ring_device(self.place + self.n + ahead, self.n)
+        span = pl.ds((way * self.cuts + cut) * self.rows, self.rows)
+        land = self.o_ref.at[origin, span]
+        return remote(
+            land,
+            land,
+            self.send_sem.at[way, step, cut],
+            self.recv_sem.at[way, step, cut],
+            {"fsdp": self.ways[way]},
+        )
+
+    def each(self):
+        return [(cut, way) for cut in range(self.cuts) for way in range(2)]
+
+    def step(self, step):
+        for cut, way in self.each():
+            if step > 0:
+                self.arrival(step - 1, cut, way).wait_recv()
+            if step < self.n - 1:
+                self.hop(step, cut, way).start()
+
+    def finish(self):
+        self.step(self.n - 1)
+        for step in range(self.n - 1):
+            for cut, way in self.each():
+                self.hop(step, cut, way).wait_send()
+        self.own().wait()
+
+
+def ring_sems(n, cuts):
+    return [
+        pltpu.SemaphoreType.DMA,
+        pltpu.SemaphoreType.DMA((2, n - 1, cuts)),
+        pltpu.SemaphoreType.DMA((2, n - 1, cuts)),
+    ]
+
+
+def ring_kernel(n, cuts, x_ref, o_ref, *sems):
+    ring = Ring(n, cuts, x_ref, o_ref, sems)
+    barrier = pltpu.get_barrier_semaphore()
+    for way in ring.ways:
+        pl.semaphore_signal(
+            barrier, inc=1, device_id={"fsdp": way}, device_id_type=pl.DeviceIdType.MESH
+        )
+    pl.semaphore_wait(barrier, 2)
+    ring.own().start()
+    for step in range(n - 1):
+        ring.step(step)
+    ring.finish()
+
+
+def ring_gather(shard, n, collective_id, cuts=2):
+    return pl.pallas_call(
+        functools.partial(ring_kernel, n, cuts),
+        out_shape=jax.ShapeDtypeStruct((n,) + shard.shape, shard.dtype),
+        in_specs=[pl.BlockSpec(memory_space=pl.ANY)],
+        out_specs=pl.BlockSpec(memory_space=pl.ANY),
+        scratch_shapes=ring_sems(n, cuts),
+        cost_estimate=pl.CostEstimate(
+            flops=0, bytes_accessed=shard.size * n * 20, transcendentals=0
+        ),
+        compiler_params=pltpu.CompilerParams(
+            collective_id=collective_id, has_side_effects=True
+        ),
+    )(shard)
+
+
+def exchange_kernel(
+    n, m, cuts, w_ref, a_ref, w_all, a_row, a_col, ring_local, ring_send, ring_recv,
+    local, head_send, head_recv, part_send, part_recv, share_send, share_recv,
+):
+    f, t = lax.axis_index("fsdp"), lax.axis_index("tp")
+    ring = Ring(n, cuts, w_ref, w_all, (ring_local, ring_send, ring_recv))
+    barrier = pltpu.get_barrier_semaphore()
+    for k in range(1, n):
+        pl.semaphore_signal(
+            barrier, inc=1, device_id={"fsdp": (f + k) % n},
+            device_id_type=pl.DeviceIdType.MESH,
+        )
+    for k in range(1, m):
+        pl.semaphore_signal(
+            barrier, inc=1, device_id={"tp": (t + k) % m},
+            device_id_type=pl.DeviceIdType.MESH,
+        )
+    pl.semaphore_wait(barrier, n + m - 2)
+    tokens, heads = a_ref.shape
+    wide = a_col.shape[2]
+    part = tokens // m
+
+    def columns(owner):
+        return a_row.at[:, pl.ds(pl.multiple_of(owner * heads, 128), heads)]
+
+    def piece(target):
+        return a_row.at[
+            pl.ds(pl.multiple_of(t * part, part), part),
+            pl.ds(pl.multiple_of(target * wide, 128), wide),
+        ]
+
+    def slot(group, quarter):
+        return a_col.at[group, pl.ds(pl.multiple_of(quarter * part, part), part)]
+
+    def share(quarter):
+        return a_col.at[:, pl.ds(pl.multiple_of(quarter * part, part), part)]
+
+    own_heads = pltpu.make_async_copy(a_ref, columns(t), local.at[0])
+    own_heads.start()
+    for k in range(1, m):
+        remote(
+            a_ref, columns(t), head_send.at[k - 1], head_recv.at[k - 1],
+            {"tp": (t + k) % m},
+        ).start()
+    ring.own().start()
+    ring.step(0)
+    own_heads.wait()
+    for k in range(1, m):
+        land = columns((t + m - k) % m)
+        remote(
+            land, land, head_send.at[k - 1], head_recv.at[k - 1], {"tp": (t + k) % m}
+        ).wait_recv()
+    own_part = pltpu.make_async_copy(piece(f), slot(f, t), local.at[1])
+    own_part.start()
+    for k in range(1, n):
+        remote(
+            piece((f + k) % n), slot(f, t), part_send.at[k - 1], part_recv.at[k - 1],
+            {"fsdp": (f + k) % n},
+        ).start()
+    ring.step(1)
+    own_part.wait()
+    for k in range(1, n):
+        land = slot((f + n - k) % n, t)
+        remote(
+            land, land, part_send.at[k - 1], part_recv.at[k - 1],
+            {"fsdp": (f + k) % n},
+        ).wait_recv()
+    for k in range(1, m):
+        remote(
+            share(t), share(t), share_send.at[k - 1], share_recv.at[k - 1],
+            {"tp": (t + k) % m},
+        ).start()
+    for step in range(2, n - 1):
+        ring.step(step)
+    ring.finish()
+    for k in range(1, m):
+        land = share((t + m - k) % m)
+        remote(
+            land, land, share_send.at[k - 1], share_recv.at[k - 1],
+            {"tp": (t + k) % m},
+        ).wait_recv()
+    for k in range(1, m):
+        remote(
+            a_ref, columns(t), head_send.at[k - 1], head_recv.at[k - 1],
+            {"tp": (t + k) % m},
+        ).wait_send()
+        remote(
+            share(t), share(t), share_send.at[k - 1], share_recv.at[k - 1],
+            {"tp": (t + k) % m},
+        ).wait_send()
+    for k in range(1, n):
+        remote(
+            piece((f + k) % n), slot(f, t), part_send.at[k - 1], part_recv.at[k - 1],
+            {"fsdp": (f + k) % n},
+        ).wait_send()
+
+
+def exchange(weights, attended, n, m, collective_id, cuts=2):
+    tokens, heads = attended.shape
+    dma = pltpu.SemaphoreType.DMA
+    return pl.pallas_call(
+        functools.partial(exchange_kernel, n, m, cuts),
+        out_shape=(
+            jax.ShapeDtypeStruct((n,) + weights.shape, weights.dtype),
+            jax.ShapeDtypeStruct((tokens, heads * m), attended.dtype),
+            jax.ShapeDtypeStruct((n, tokens, heads * m // n), attended.dtype),
+        ),
+        in_specs=[pl.BlockSpec(memory_space=pl.ANY)] * 2,
+        out_specs=[pl.BlockSpec(memory_space=pl.ANY)] * 3,
+        scratch_shapes=ring_sems(n, cuts)
+        + [dma((2,))]
+        + [dma((m - 1,))] * 2
+        + [dma((n - 1,))] * 2
+        + [dma((m - 1,))] * 2,
+        cost_estimate=pl.CostEstimate(
+            flops=0, bytes_accessed=weights.size * n * 20, transcendentals=0
+        ),
+        compiler_params=pltpu.CompilerParams(
+            collective_id=collective_id, has_side_effects=True
+        ),
+    )(weights, attended)
+
+
+def shards(fsdp, tp, step_input, lengths, cache_k, cache_v, w_query, w_key, w_value, w_output, loss_grad):
     steps, rows, width = step_input.shape
     flat = step_input.reshape(steps * rows, width)
     head_size = HD
     kv_local = w_key.shape[1] // head_size
     q_local = w_query.shape[1] // head_size
     group = q_local // kv_local
-    out_whole = lax.all_gather(w_output, "fsdp", axis=0, tiled=True)
-    q_full, k_full, v_full = (
-        lax.all_gather(w_query, "fsdp", axis=0, tiled=True),
-        lax.all_gather(w_key, "fsdp", axis=0, tiled=True),
-        lax.all_gather(w_value, "fsdp", axis=0, tiled=True),
-    )
-    query = jnp.dot(flat, q_full, preferred_element_type=jnp.float32)
-    key = jnp.dot(flat, k_full, preferred_element_type=jnp.float32)
-    value = jnp.dot(flat, v_full, preferred_element_type=jnp.float32)
+    upstream = loss_grad.reshape(steps * rows, loss_grad.shape[2])
+    fused = jnp.concatenate([w_query, w_key, w_value], axis=1)
+    weights, upstream = lax.optimization_barrier((ring_gather(fused, fsdp, 0), upstream))
+    weights = weights.reshape(width, fused.shape[1])
+    grad_whole = lax.all_gather(upstream, "fsdp", axis=0, tiled=True)
+    projection = jnp.dot(flat, weights, preferred_element_type=jnp.float32)
+    query, key, value = jnp.split(
+        projection, (w_query.shape[1], w_query.shape[1] + w_key.shape[1]), axis=1
+    )
     pos = lengths.astype(jnp.float32)[None, :] + jnp.arange(steps).astype(jnp.float32)[:, None]
     q_rot = rotate(query.reshape(steps, rows, q_local, head_size), pos[:, :, None]).astype(
         jnp.bfloat16
@@ -72,17 +317,13 @@
     )
     v_new = value.reshape(steps, rows, kv_local, head_size).astype(jnp.bfloat16)
     local_attended = attend(q_rot, k_new, v_new, cache_k, cache_v, lengths, kv_local, group)
-    attended = lax.all_gather(local_attended, "tp", axis=1, tiled=True)
+    out_whole, attended, swapped = exchange(w_output, local_attended, fsdp, tp, 1)
+    out_whole = out_whole.reshape(attended.shape[1], w_output.shape[1])
+    swapped = swapped.reshape(fsdp * steps * rows, swapped.shape[2])
     projected = jnp.dot(attended, out_whole, preferred_element_type=jnp.float32)
     layer_out = projected.astype(jnp.bfloat16).reshape(steps, rows, w_output.shape[1])
-    upstream = loss_grad.reshape(steps * rows, loss_grad.shape[2])
-    grad_output = lax.psum_scatter(
-        lax.dot_general(
-            attended, upstream, (((0,), (0,)), ((), ())), preferred_element_type=jnp.float32
-        ),
-        "fsdp",
-        scatter_dimension=0,
-        tiled=True,
+    grad_output = lax.dot_general(
+        swapped, grad_whole, (((0,), (0,)), ((), ())), preferred_element_type=jnp.float32
     )
     return (layer_out, grad_output)
 
@@ -100,4 +341,5 @@
         P(None, "fsdp", "tp"),
     )
     out_specs = (P(None, "fsdp", "tp"), P("fsdp", "tp"))
-    return jax.shard_map(shards, mesh=mesh, in_specs=in_specs, out_specs=out_specs, check_vma=False)
+    body = functools.partial(shards, mesh.shape["fsdp"], mesh.shape["tp"])
+    return jax.shard_map(body, mesh=mesh, in_specs=in_specs, out_specs=out_specs, check_vma=False)

time: 1270 us -> 630 us (0.50)
  waiting for transfers between devices: 1110 us -> 0.02 us
  Pallas kernels: 0 us -> 505 us
  local copies, waits for them, and re-layouts: 66.1 us -> 34.8 us
    all_gather x5 -> x1, waiting for transfers between devices: 570 us -> 0.01 us  [shards(): grad_whole = lax.all_gather(upstream, 'fsdp', axis=0, tiled=True)]
    reduce_scatter x1 -> x0, waiting for transfers between devices: 534 us -> none  [shards(): lax.psum_scatter(lax.dot_general(attended, upstream, (((0,), (0,)), ((),...]
    pallas_call x0 -> x2, Pallas kernels: none -> 505 us  [the longest x1 264 us: exchange(): pl.pallas_call(functools.partial(exchange_kernel, n, m, cuts), out_shape=...]
    dot_general x3 -> x0, local copies, waits for them, and re-layouts: 33.7 us -> none  [the longest x1 21 us: shards(): query = jnp.dot(flat, q_full, preferred_element_type=jnp.float32)]
    dot_general x4 -> x2, matrix products: 40.6 us -> 29.5 us  [the longest x1 18.5 us: shards(): projection = jnp.dot(flat, weights, preferred_element_type=jnp.float32)]
  transfers between devices with their start and end apart: 6 -> 1, of which waited for: 6 -> 0; matrix products, arithmetic and copies ran while one was open for 6% -> 14% of each run, Pallas kernels for 0% -> 42%
where the time goes in v1:
time: 630 us; the launch traced here: 626 us
  Pallas kernels  505 us (80%)
  matrix products  62.8 us (10%)
  local copies, waits for them, and re-layouts  34.8 us (6%)
  between operations  14.3 us (2%)
  other arithmetic  8.35 us (1%)
    pallas_call x1, Pallas kernels, exchange(): pl.pallas_call(functools.partial(exchange_kernel, n, m, cuts), out_shape=...  264 us
    pallas_call x1, Pallas kernels, ring_gather(): pl.pallas_call(functools.partial(ring_kernel, n, cuts), out_shape=jax.Sha...  242 us
    dot_general x1, matrix products, shards(): projection = jnp.dot(flat, weights, preferred_element_type=jnp.float32)  18.5 us
  transfers between devices with their start and end apart: 1, of which 0 were waited for; matrix products, arithmetic and copies ran while one was open for 14% of the time, Pallas kernels for 42%

profile of v1, /device:TPU:0, one launch (start us, length us, event | category | flops | bytes accessed | tf_op | source)
XLA Modules:
  0.0 625.8 jit_solution(3137038598218752892)
XLA Ops:
  7.2 3.2 pad_maximum_fusion.x_ref
  10.4 241.8 %shard_map.104 = bf16[8,1024,1536]{2,1,0:T(8,128)(2,1)} custom-call(bf16[1024,1536]{1,0:T(8,128)(2,1)} %pad_maximum_fusion.x_ref), custom_call_target="tpu_custom_call" | custom-call | bytes 251658240 | tf_op jit(solution)/shard_map/pallas_call | solution.py:157
  252.2 18.5 %convolution_bitcast_fusion = f32[384,1536]{0,1:T(8,128)S(1)} fusion(bf16[8192,1536]{1,0:T(8,128)(2,1)} %bitcast.61, bf16[384,8192]{1,0:T(8,128)(2,1)} %bitcast.71), kind=kOutput, calls=%fused_computation.5 | convolution fusion | flops 9663676416 | bytes 33816576 | tf_op jit(solution)/shard_map/dot_general | solution.py:307
  270.9 1.3 copy-done
  272.2 0.5 multiply_cosine_fusion
  272.8 0.8 copy.79
  273.6 0.8 copy.88
  274.4 0.8 copy.80
  275.2 0.8 copy.90
  275.9 1.7 split.17
  277.6 0.5 copy.78
  278.1 0.3 copy.122
  278.4 0.6 slice-done
  279.1 0.3 reshape.148
  279.9 0.4 copy-done.2
  280.4 0.6 subtract_convert_fusion
  281.1 1.1 pad_maximum_fusion.1
  282.4 7.0 %fusion.14 = f32[96,2,4,4,4]{4,2,3,1,0:T(4,128)S(1)} fusion(bf16[4,96,2,4,128]{4,3,2,1,0:T(4,128)(2,1)S(1)} %pad_maximum_fusion.1, bf16[4,96,2,64]{3,0,2,1:T(4,128)(2,1)S(1)} %get-tuple-element.15, bf16[4,96,2,64]{3,0,2,1:T(4,128)(2,1)S(1)} %get-tuple-element.14), kind=kOutput, calls=%fused_computation.23 | convolution fusion | flops 3538944 | bytes 1032192 | tf_op jit(solution)/shard_map/srhgd,trhd->srhgt/dot_general | solution.py:38
  289.4 0.8 copy.91
  290.6 9.9 %reshape.136 = bf16[96,128,2,128]{3,2,1,0:T(2,128)(2,1)} reshape(bf16[96,128,256]{2,1,0:T(8,128)(2,1)} %param.11) | data formatting | bytes 12582912 | tf_op jit(solution)/shard_map/reshape | solution.py:34
  300.6 7.4 %bitcast_reduce_fusion = (f32[4,96,2,4]{3,0,2,1:T(4,128)S(1)}, f32[96,2,4,4,128]{4,3,2,1,0:T(4,128)}) fusion(bf16[96,128,2,128,1]{3,2,1,0,4:T(2,128)(2,1)} %bitcast.64, bf16[4,96,2,4,128]{4,3,2,1,0:T(4,128)(2,1)S(1)} %pad_maximum_fusion.1, pred[96,128]{1,0:T(8,128)(4,1)S(1)} %iota_compare_fusion), kind=kOutput, calls=%fused_computation.10 | convolution fusion | flops 101839872 | bytes 8675328 | tf_op jit(solution)/shard_map/srhgd,rchd->srhgc/dot_general | solution.py:37
  308.8 0.7 copy-done.1
  309.5 1.9 fusion.9
  311.9 1.5 copy.99
  313.3 10.0 %reshape.138 = bf16[96,128,2,128]{3,2,1,0:T(2,128)(2,1)} reshape(bf16[96,128,256]{2,1,0:T(8,128)(2,1)} %param.12) | data formatting | bytes 12582912 | tf_op jit(solution)/shard_map/reshape | solution.py:35
  323.7 5.8 fusion
  329.6 0.7 fusion.4
  330.3 0.3 copy.100
  330.5 1.4 reshape.139.a_ref
  332.0 263.6 %shard_map.105 = (bf16[8,512,2048]{2,1,0:T(8,128)(2,1)}, bf16[384,4096]{1,0:T(8,128)(2,1)}, bf16[8,384,512]{2,1,0:T(8,128)(2,1)}) custom-call(bf16[512,2048]{1,0:T(8,128)(2,1)} %w_ref.1, bf16[384,1024]{1,0:T(8,128)(2,1)} %reshape.139.a_ref), custom_call_target="tpu_custom_call" | custom-call | bytes 167772160 | tf_op jit(solution)/shard_map/pallas_call | solution.py:272
  595.6 12.4 %convolution_convert_fusion = bf16[384,2048]{1,0:T(8,128)(2,1)} fusion(bf16[384,4096]{1,0:T(8,128)(2,1)} %get-tuple-element.8, bf16[4096,2048]{1,0:T(8,128)(2,1)} %bitcast.70), kind=kOutput, calls=%fused_computation.6 | convolution fusion | flops 6443237376 | bytes 21495808 | tf_op jit(solution)/shard_map/dot_general | solution.py:323
  608.0 11.0 %fusion.24 = f32[512,2048]{1,0:T(8,128)} fusion(bf16[3072,512]{1,0:T(8,128)(2,1)S(1)} %bitcast.72, bf16[3072,2048]{1,0:T(8,128)(2,1)} %all-gather.2.cloned.1.call-done), kind=kOutput, calls=%fused_computation.47 | convolution fusion | flops 6442450944 | bytes 19922944 | tf_op jit(solution)/shard_map/dot_general | solution.py:325
  (43 shorter events, 3.0 us)
Async XLA Ops:
  7.2 600.8 %all-gather.2.cloned.1.call-start = ((), (), s32[]{:S(2)}) async-start(), calls=%async_computation | async-start | bytes 14155776 | tf_op jit(solution)/shard_map/all_gather | solution.py:306
  270.7 1.4 copy-start
  270.8 1.4 copy-start.8
  278.1 1.0 slice-start
  279.4 0.9 copy-start.2
  279.4 1.0 copy-start.3
  281.1 1.1 copy-start.5
  281.1 1.1 copy-start.6
  308.1 1.4 copy-start.1
  313.3 10.0 %copy-start.4 = (bf16[384,256]{0,1:T(8,128)(2,1)S(1)}, bf16[384,256]{0,1:T(8,128)(2,1)}, u32[]{:S(2)}) copy-start(bf16[384,256]{0,1:T(8,128)(2,1)} %split.17) | copy-start | bytes 589828
  323.7 5.9 copy-start.7
  595.6 12.4 %copy-start.9 = (bf16[8,384,512]{2,1,0:T(8,128)(2,1)S(1)}, bf16[8,384,512]{2,1,0:T(8,128)(2,1)}, u32[]{:S(2)}) copy-start(bf16[8,384,512]{2,1,0:T(8,128)(2,1)} %get-tuple-element.10) | copy-start | bytes 9437188
Sparse Core Ops, SparseCore 0:
  252.3 260.5 all-gather.1

commit v2 on v1

--- a/solution.py
+++ b/solution.py
@@ -74,7 +74,8 @@
 
 
 class Ring:
-    def __init__(self, n, cuts, x_ref, o_ref, sems):
+    def __init__(self, n, cuts, x_ref, o_ref, sems, early=()):
+        self.early, self.begin = early, len(early)
         self.n, self.cuts, self.x_ref, self.o_ref = n, cuts, x_ref, o_ref
         self.local_sem, self.send_sem, self.recv_sem = sems
         self.me = lax.axis_index("fsdp")
@@ -92,8 +93,11 @@
         origin = ring_device(self.place + self.n + (step if way else -step), self.n)
         span = pl.ds((way * self.cuts + cut) * self.rows, self.rows)
         land = self.o_ref.at[origin, span]
+        source = self.x_ref.at[span] if step == 0 else land
+        if step == self.begin and step > 0:
+            source = self.early[step - 1][way].at[pl.ds(cut * self.rows, self.rows)]
         return remote(
-            self.x_ref.at[span] if step == 0 else land,
+            source,
             land,
             self.send_sem.at[way, step, cut],
             self.recv_sem.at[way, step, cut],
@@ -113,22 +117,34 @@
             {"fsdp": self.ways[way]},
         )
 
+    def keep(self, sem):
+        copies = [pltpu.make_async_copy(self.x_ref, self.o_ref.at[self.me], sem.at[0, 0])]
+        for step, pair in enumerate(self.early):
+            for way in range(2):
+                ahead = step + 1 if way else -step - 1
+                origin = ring_device(self.place + self.n + ahead, self.n)
+                span = pl.ds(way * self.cuts * self.rows, self.cuts * self.rows)
+                copies.append(
+                    pltpu.make_async_copy(
+                        pair[way], self.o_ref.at[origin, span], sem.at[step + 1, way]
+                    )
+                )
+        return copies
+
     def each(self):
         return [(cut, way) for cut in range(self.cuts) for way in range(2)]
 
     def step(self, step):
         for cut, way in self.each():
-            if step > 0:
+            if step > self.begin:
                 self.arrival(step - 1, cut, way).wait_recv()
             if step < self.n - 1:
                 self.hop(step, cut, way).start()
 
     def finish(self):
-        self.step(self.n - 1)
-        for step in range(self.n - 1):
+        for step in range(self.begin, self.n - 1):
             for cut, way in self.each():
                 self.hop(step, cut, way).wait_send()
-        self.own().wait()
 
 
 def ring_sems(n, cuts):
@@ -150,7 +166,9 @@
     ring.own().start()
     for step in range(n - 1):
         ring.step(step)
+    ring.step(n - 1)
     ring.finish()
+    ring.own().wait()
 
 
 def ring_gather(shard, n, collective_id, cuts=2):
@@ -169,12 +187,18 @@
     )(shard)
 
 
-def exchange_kernel(
-    n, m, cuts, w_ref, a_ref, w_all, a_row, a_col, ring_local, ring_send, ring_recv,
-    local, head_send, head_recv, part_send, part_recv, share_send, share_recv,
-):
+def exchange_kernel(n, m, cuts, early, w_ref, g_ref, a_ref, *refs):
+    w_early = [refs[2 * k : 2 * k + 2] for k in range(early)]
+    g_early = [refs[2 * k : 2 * k + 2] for k in range(early, 2 * early)]
+    (
+        out_ref, w_all, g_all, a_row, a_col,
+        ring_local, ring_send, ring_recv, g_local, g_send, g_recv,
+        local, head_send, head_recv, part_send, part_recv, share_send, share_recv,
+        held, block, total, load, keep_sem,
+    ) = refs[4 * early :]
     f, t = lax.axis_index("fsdp"), lax.axis_index("tp")
-    ring = Ring(n, cuts, w_ref, w_all, (ring_local, ring_send, ring_recv))
+    ring = Ring(n, cuts, w_ref, w_all, (ring_local, ring_send, ring_recv), w_early)
+    ring_g = Ring(n, cuts, g_ref, g_all, (g_local, g_send, g_recv), g_early)
     barrier = pltpu.get_barrier_semaphore()
     for k in range(1, n):
         pl.semaphore_signal(
@@ -206,6 +230,41 @@
     def share(quarter):
         return a_col.at[:, pl.ds(pl.multiple_of(quarter * part, part), part)]
 
+    half = w_ref.shape[0] // 2
+    tile = min(512, total.shape[1])
+
+    def multiply(origin, sources):
+        copies = [
+            pltpu.make_async_copy(source, block.at[way], load.at[way])
+            for way, source in enumerate(sources)
+        ]
+        for copy in copies:
+            copy.start()
+        for way, copy in enumerate(copies):
+            copy.wait()
+            depth = pl.ds(
+                pl.multiple_of(origin[way] * 2 * half + way * half, 128), half
+            )
+
+            @pl.loop(0, total.shape[1] // tile)
+            def _(j):
+                span = pl.ds(pl.multiple_of(j * tile, 128), tile)
+                total[:, span] += jnp.dot(
+                    held[:, depth], block[way, :, span],
+                    preferred_element_type=jnp.float32,
+                )
+
+    def arrived(step):
+        ends = [
+            ring_device(ring.place + n + (step + 1 if way else -step - 1), n)
+            for way in range(2)
+        ]
+        if step < early:
+            return ends, w_early[step]
+        return ends, [
+            w_all.at[end, pl.ds(way * half, half)] for way, end in enumerate(ends)
+        ]
+
     own_heads = pltpu.make_async_copy(a_ref, columns(t), local.at[0])
     own_heads.start()
     for k in range(1, m):
@@ -213,8 +272,11 @@
             a_ref, columns(t), head_send.at[k - 1], head_recv.at[k - 1],
             {"tp": (t + k) % m},
         ).start()
-    ring.own().start()
-    ring.step(0)
+    ring.step(early)
+    ring_g.step(early)
+    kept = ring_g.keep(keep_sem)
+    for copy in kept:
+        copy.start()
     own_heads.wait()
     for k in range(1, m):
         land = columns((t + m - k) % m)
@@ -228,7 +290,13 @@
             piece((f + k) % n), slot(f, t), part_send.at[k - 1], part_recv.at[k - 1],
             {"fsdp": (f + k) % n},
         ).start()
-    ring.step(1)
+    rows_in = pltpu.make_async_copy(a_row, held, local.at[2])
+    rows_in.start()
+    total[...] = jnp.zeros_like(total)
+    rows_in.wait()
+    multiply([f, f], [w_ref.at[pl.ds(way * half, half)] for way in range(2)])
+    for step in range(early):
+        multiply(*arrived(step))
     own_part.wait()
     for k in range(1, n):
         land = slot((f + n - k) % n, t)
@@ -241,9 +309,15 @@
             share(t), share(t), share_send.at[k - 1], share_recv.at[k - 1],
             {"tp": (t + k) % m},
         ).start()
-    for step in range(2, n - 1):
+    for step in range(early + 1, n):
         ring.step(step)
+        ring_g.step(step)
+        multiply(*arrived(step - 1))
+    out_ref[...] = total[...].astype(out_ref.dtype)
     ring.finish()
+    ring_g.finish()
+    for copy in kept:
+        copy.wait()
     for k in range(1, m):
         land = share((t + m - k) % m)
         remote(
@@ -266,30 +340,45 @@
         ).wait_send()
 
 
-def exchange(weights, attended, n, m, collective_id, cuts=2):
+def exchange(weights, upstream, attended, w_early, g_early, n, m, collective_id, cuts=2):
     tokens, heads = attended.shape
+    half, wide = weights.shape[0] // 2, weights.shape[1]
+    early = len(w_early)
     dma = pltpu.SemaphoreType.DMA
-    return pl.pallas_call(
-        functools.partial(exchange_kernel, n, m, cuts),
+    anywhere = pl.BlockSpec(memory_space=pl.ANY)
+    out, _, grad_whole, _, swapped = pl.pallas_call(
+        functools.partial(exchange_kernel, n, m, cuts, early),
         out_shape=(
+            jax.ShapeDtypeStruct((tokens, wide), attended.dtype),
             jax.ShapeDtypeStruct((n,) + weights.shape, weights.dtype),
+            jax.ShapeDtypeStruct((n,) + upstream.shape, upstream.dtype),
             jax.ShapeDtypeStruct((tokens, heads * m), attended.dtype),
             jax.ShapeDtypeStruct((n, tokens, heads * m // n), attended.dtype),
         ),
-        in_specs=[pl.BlockSpec(memory_space=pl.ANY)] * 2,
-        out_specs=[pl.BlockSpec(memory_space=pl.ANY)] * 3,
-        scratch_shapes=ring_sems(n, cuts)
-        + [dma((2,))]
+        in_specs=[anywhere] * (3 + 4 * early),
+        out_specs=[pl.BlockSpec(memory_space=pltpu.VMEM)] + [anywhere] * 4,
+        scratch_shapes=ring_sems(n, cuts) * 2
+        + [dma((3,))]
         + [dma((m - 1,))] * 2
         + [dma((n - 1,))] * 2
-        + [dma((m - 1,))] * 2,
+        + [dma((m - 1,))] * 2
+        + [
+            pltpu.VMEM((tokens, heads * m), attended.dtype),
+            pltpu.VMEM((2, half, wide), weights.dtype),
+            pltpu.VMEM((tokens, wide), jnp.float32),
+            dma((2,)),
+            dma((early + 1, 2)),
+        ],
         cost_estimate=pl.CostEstimate(
             flops=0, bytes_accessed=weights.size * n * 20, transcendentals=0
         ),
         compiler_params=pltpu.CompilerParams(
-            collective_id=collective_id, has_side_effects=True
+            collective_id=collective_id,
+            has_side_effects=True,
+            vmem_limit_bytes=32 * 1024 * 1024,
         ),
-    )(weights, attended)
+    )(weights, upstream, attended, *sum(w_early, ()), *sum(g_early, ()))
+    return out, grad_whole, swapped
 
 
 def shards(fsdp, tp, step_input, lengths, cache_k, cache_v, w_query, w_key, w_value, w_output, loss_grad):
@@ -301,9 +390,20 @@
     group = q_local // kv_local
     upstream = loss_grad.reshape(steps * rows, loss_grad.shape[2])
     fused = jnp.concatenate([w_query, w_key, w_value], axis=1)
-    weights, upstream = lax.optimization_barrier((ring_gather(fused, fsdp, 0), upstream))
+    w_halves, g_halves = tuple(jnp.split(w_output, 2)), tuple(jnp.split(upstream, 2))
+    weights, w_halves, g_halves = lax.optimization_barrier(
+        (ring_gather(fused, fsdp, 0), w_halves, g_halves)
+    )
+    order = [ring_device(place, fsdp) for place in range(fsdp)]
+    after = order[1:] + order[:1]
+    pairs = (list(zip(order, after)), list(zip(after, order)))
+    w_early, g_early = [], []
+    for _ in range(2):
+        w_halves = tuple(lax.ppermute(h, "fsdp", p) for h, p in zip(w_halves, pairs))
+        g_halves = tuple(lax.ppermute(h, "fsdp", p) for h, p in zip(g_halves, pairs))
+        w_early.append(w_halves)
+        g_early.append(g_halves)
     weights = weights.reshape(width, fused.shape[1])
-    grad_whole = lax.all_gather(upstream, "fsdp", axis=0, tiled=True)
     projection = jnp.dot(flat, weights, preferred_element_type=jnp.float32)
     query, key, value = jnp.split(
         projection, (w_query.shape[1], w_query.shape[1] + w_key.shape[1]), axis=1
@@ -317,11 +417,12 @@
     )
     v_new = value.reshape(steps, rows, kv_local, head_size).astype(jnp.bfloat16)
     local_attended = attend(q_rot, k_new, v_new, cache_k, cache_v, lengths, kv_local, group)
-    out_whole, attended, swapped = exchange(w_output, local_attended, fsdp, tp, 1)
-    out_whole = out_whole.reshape(attended.shape[1], w_output.shape[1])
+    layer_out, grad_whole, swapped = exchange(
+        w_output, upstream, local_attended, w_early, g_early, fsdp, tp, 1
+    )
+    grad_whole = grad_whole.reshape(fsdp * steps * rows, upstream.shape[1])
+    layer_out = layer_out.reshape(steps, rows, w_output.shape[1])
     swapped = swapped.reshape(fsdp * steps * rows, swapped.shape[2])
-    projected = jnp.dot(attended, out_whole, preferred_element_type=jnp.float32)
-    layer_out = projected.astype(jnp.bfloat16).reshape(steps, rows, w_output.shape[1])
     grad_output = lax.dot_general(
         swapped, grad_whole, (((0,), (0,)), ((), ())), preferred_element_type=jnp.float32
     )

time: 630 us -> 598 us (0.949)
  Pallas kernels: 505 us -> 465 us
  waiting for transfers between devices: 0.02 us -> 24.6 us
  between operations: 14.3 us -> 0.95 us
  matrix products: 62.8 us -> 49.5 us
  starting transfers between devices: 0.04 us -> 8.21 us
  local copies, waits for them, and re-layouts: 34.8 us -> 42 us
    pallas_call x1, Pallas kernels: 264 us -> 223 us  [exchange(): pl.pallas_call(functools.partial(exchange_kernel, n, m, cuts, early), out...]
    ppermute x0 -> x8, waiting for transfers between devices: none -> 24.6 us  [shards(): lax.ppermute(h, 'fsdp', p)]
    dot_general x1 -> x0, matrix products: 12.4 us -> none  [shards(): projected = jnp.dot(attended, out_whole, preferred_element_type=jnp.float32)]
    ppermute x0 -> x8, starting transfers between devices: none -> 8.21 us  [shards(): lax.ppermute(h, 'fsdp', p)]
  transfers between devices with their start and end apart: 1 -> 8, of which waited for: 0 -> 4; matrix products, arithmetic and copies ran while one was open for 14% -> 13% of each run, Pallas kernels for 42% -> 0%
where the time goes in v2:
time: 598 us; the launch traced here: 597 us
  Pallas kernels  465 us (78%)
  matrix products  49.5 us (8%)
  local copies, waits for them, and re-layouts  42 us (7%)
  waiting for transfers between devices  24.6 us (4%)
  starting transfers between devices  8.21 us (1%)
  other arithmetic  6.91 us (1%)
    pallas_call x1, Pallas kernels, ring_gather(): pl.pallas_call(functools.partial(ring_kernel, n, cuts), out_shape=jax.Sha...  242 us
    pallas_call x1, Pallas kernels, exchange(): pl.pallas_call(functools.partial(exchange_kernel, n, m, cuts, early), out...  223 us
    ppermute x8, waiting for transfers between devices, shards(): lax.ppermute(h, 'fsdp', p)  24.6 us
    dot_general x1, matrix products, shards(): projection = jnp.dot(flat, weights, preferred_element_type=jnp.float32)  18.5 us
  transfers between devices with their start and end apart: 8, of which 4 were waited for; matrix products, arithmetic and copies ran while one was open for 13% of the time, Pallas kernels for 0%

profile of v2, /device:TPU:0, one launch (start us, length us, event | category | flops | bytes accessed | tf_op | source)
XLA Modules:
  0.0 596.7 jit_solution(16244403062938532991)
XLA Ops:
  0.6 3.3 fusion.23
  4.0 1.2 fusion.24
  5.2 0.9 copy-done.6
  6.3 1.8 pad_maximum_fusion.x_ref
  8.1 241.8 %shard_map.104 = bf16[8,1024,1536]{2,1,0:T(8,128)(2,1)} custom-call(bf16[1024,1536]{1,0:T(8,128)(2,1)} %pad_maximum_fusion.x_ref), custom_call_target="tpu_custom_call" | custom-call | bytes 251658240 | tf_op jit(solution)/shard_map/pallas_call | solution.py:175
  249.9 1.6 collective-permute-start
  252.0 1.6 collective-permute-start.4
  254.0 18.5 %convolution_bitcast_fusion.1 = f32[384,1536]{0,1:T(8,128)S(1)} fusion(bf16[8192,1536]{1,0:T(8,128)(2,1)} %bitcast.63, bf16[384,8192]{1,0:T(8,128)(2,1)} %bitcast.71), kind=kOutput, calls=%fused_computation.6 | convolution fusion | flops 9663676416 | bytes 33816576 | tf_op jit(solution)/shard_map/dot_general | solution.py:407
  272.6 1.4 copy-done.4
  276.5 1.6 copy.82
  278.1 1.8 copy.128
  280.8 9.7 %reshape.134 = bf16[96,128,2,128]{3,2,1,0:T(2,128)(2,1)} reshape(bf16[96,128,256]{2,1,0:T(8,128)(2,1)} %param.11) | data formatting | bytes 12582912 | tf_op jit(solution)/shard_map/reshape | solution.py:34
  291.1 1.1 pad_maximum_fusion.1
  292.2 1.1 copy-done.3
  293.3 4.6 bitcast_reduce_fusion
  298.1 7.0 %fusion.14 = f32[96,2,4,4,4]{4,2,3,1,0:T(4,128)S(1)} fusion(bf16[4,96,2,4,128]{4,3,2,1,0:T(4,128)(2,1)S(1)} %pad_maximum_fusion.1, bf16[4,96,2,64]{3,0,2,1:T(4,128)(2,1)S(1)} %get-tuple-element.25, bf16[4,96,2,64]{3,0,2,1:T(4,128)(2,1)S(1)} %get-tuple-element.24), kind=kOutput, calls=%fused_computation.23 | convolution fusion | flops 3538944 | bytes 1032192 | tf_op jit(solution)/shard_map/srhgd,trhd->srhgt/dot_general | solution.py:38
  307.0 9.8 %reshape.136 = bf16[96,128,2,128]{3,2,1,0:T(2,128)(2,1)} reshape(bf16[96,128,256]{2,1,0:T(8,128)(2,1)} %param.12) | data formatting | bytes 12582912 | tf_op jit(solution)/shard_map/reshape | solution.py:35
  316.8 1.9 fusion.9
  318.9 1.6 collective-permute-start.6
  321.0 1.6 collective-permute-start.2
  323.0 6.3 %fusion = f32[96,2,4,4,128]{4,3,2,1,0:T(4,128)} fusion(bf16[96,128,2,128,1]{3,2,1,0,4:T(2,128)(2,1)} %bitcast.65, f32[96,2,4,4,128]{4,3,2,1,0:T(4,128)S(1)} %copy-done.8, f32[4,96,2,4]{3,0,2,1:T(4,128)S(1)} %add.39, f32[4,96,2,4]{3,0,2,1:T(4,128)S(1)} %max.7, pred[96,128]{1,0:T(8,128)(4,1)S(1)} %iota_compare_fusion), kind=kOutput, calls=%fused_computation | convolution fusion | flops 102236160 | bytes 9474048 | tf_op jit(solution)/shard_map/srhgc,rchd->srhgd/dot_general | solution.py:49
  330.9 2.1 fusion.4
  333.0 1.2 copy.104
  334.1 1.6 reshape.137.a_ref
  335.8 4.0 collective-permute-done.6.refs_6_
  339.8 1.6 collective-permute-done.7.refs_7_
  341.3 17.7 %collective-permute-done.2.refs_2_ = bf16[256,2048]{1,0:T(8,128)(2,1)} collective-permute-done((bf16[256,2048]{1,0:T(8,128)(2,1)}, bf16[256,2048]{1,0:T(8,128)(2,1)}, u32[]{:S(2)}, u32[]{:S(2)}) %collective-permute-start.2) | collective-permute-done | bytes 1048608 | tf_op jit(solution)/shard_map/ppermute | solution.py:402
  359.1 1.3 collective-permute-done.3.refs_3_
  360.4 1.4 copy-done.2
  361.8 222.8 %shard_map.105 = (bf16[384,2048]{1,0:T(8,128)(2,1)S(1)}, bf16[8,512,2048]{2,1,0:T(8,128)(2,1)}, bf16[8,384,2048]{2,1,0:T(8,128)(2,1)}, bf16[384,4096]{1,0:T(8,128)(2,1)}, bf16[8,384,512]{2,1,0:T(8,128)(2,1)S(1)}) custom-call(bf16[512,2048]{1,0:T(8,128)(2,1)S(1)} %copy-done, bf16[384,2048]{1,0:T(8,128)(2,1)S(1)} %bitcast.61, ...), custom_call_target="tpu_custom_call" | custom-call | bytes 167772160 | tf_op jit(solution)/shard_map/pallas_call | solution.py:349
  584.6 11.0 %convolution_bitcast_fusion = f32[512,2048]{1,0:T(8,128)} fusion(bf16[8,384,512]{2,1,0:T(8,128)(2,1)S(1)} %get-tuple-element.16, bf16[8,384,2048]{2,1,0:T(8,128)(2,1)} %get-tuple-element.17), kind=kOutput, calls=%fused_computation.4 | convolution fusion | flops 6442450944 | bytes 19922944 | tf_op jit(solution)/shard_map/dot_general | solution.py:426
  595.6 1.1 copy.144
  (67 shorter events, 9.7 us)
Async XLA Ops:
  0.6 3.3 copy-start.1
  3.9 2.2 copy-start.6
  3.9 2.2 copy-start.11
  3.9 2.4 copy-start.12
  249.9 71.1 %collective-permute-start = (bf16[256,2048]{1,0:T(8,128)(2,1)}, bf16[256,2048]{1,0:T(8,128)(2,1)}, u32[]{:S(2)}, u32[]{:S(2)}) collective-permute-start(bf16[256,2048]{1,0:T(8,128)(2,1)} %get-tuple-element.11), channel_id=1, source_target_pairs={{0,8},{8,16},{16,24},{24,28},{28,20},{20,12},{12,4},{4,0},{1,9},{9... | collective-permute-start | bytes 3145736 | tf_op jit(solution)/shard_map/ppermute | solution.py:402
  251.6 71.0 %collective-permute-start.1 = (bf16[256,2048]{1,0:T(8,128)(2,1)}, bf16[256,2048]{1,0:T(8,128)(2,1)}, u32[]{:S(2)}, u32[]{:S(2)}) collective-permute-start(bf16[256,2048]{1,0:T(8,128)(2,1)} %get-tuple-element.12), channel_id=1, source_target_pairs={{8,0},{16,8},{24,16},{28,24},{20,28},{12,20},{4,12},{0,4},{9,1},{1... | collective-permute-start | bytes 3145736 | tf_op jit(solution)/shard_map/ppermute | solution.py:402
  252.0 66.9 %collective-permute-start.4 = (bf16[192,2048]{1,0:T(8,128)(2,1)}, bf16[192,2048]{1,0:T(8,128)(2,1)}, u32[]{:S(2)}, u32[]{:S(2)}) collective-permute-start(bf16[192,2048]{1,0:T(8,128)(2,1)} %bitcast.1), channel_id=1, source_target_pairs={{0,8},{8,16},{16,24},{24,28},{28,20},{20,12},{12,4},{4,0},{1,9},{9... | collective-permute-start | bytes 2359304 | tf_op jit(solution)/shard_map/ppermute | solution.py:403
  253.6 67.0 %collective-permute-start.5 = (bf16[192,2048]{1,0:T(8,128)(2,1)}, bf16[192,2048]{1,0:T(8,128)(2,1)}, u32[]{:S(2)}, u32[]{:S(2)}) collective-permute-start(bf16[192,2048]{1,0:T(8,128)(2,1)} %bitcast.2), channel_id=1, source_target_pairs={{8,0},{16,8},{24,16},{28,24},{20,28},{12,20},{4,12},{0,4},{9,1},{1... | collective-permute-start | bytes 2359304 | tf_op jit(solution)/shard_map/ppermute | solution.py:403
  272.5 1.4 copy-start.4
  272.6 1.4 copy-start.13
  274.0 2.5 slice-start
  278.1 1.8 slice-start.1
  290.5 2.8 copy-start.3
  293.2 4.6 copy-start.9
  293.3 4.6 copy-start.10
  307.0 9.8 %copy-start.7 = (f32[96,2,4,4,128]{4,3,2,1,0:T(4,128)S(1)}, f32[96,2,4,4,128]{4,3,2,1,0:T(4,128)}, u32[]{:S(2)}) copy-start(f32[96,2,4,4,128]{4,3,2,1,0:T(4,128)} %get-tuple-element.31) | copy-start | bytes 4718596
  316.8 6.2 %copy-start.8 = (f32[96,2,4,4,128]{4,3,2,1,0:T(4,128)S(1)}, f32[96,2,4,4,128]{4,3,2,1,0:T(4,128)}, u32[]{:S(2)}) copy-start(f32[96,2,4,4,128]{4,3,2,1,0:T(4,128)} %get-tuple-element.31) | copy-start | bytes 4718596
  318.9 20.8 %collective-permute-start.6 = (bf16[192,2048]{1,0:T(8,128)(2,1)}, bf16[192,2048]{1,0:T(8,128)(2,1)}, u32[]{:S(2)}, u32[]{:S(2)}) collective-permute-start(bf16[192,2048]{1,0:T(8,128)(2,1)} %collective-permute-done.4.refs_4_), channel_id=1, source_target_pairs={{0,8},{8,16},{16,24},{24,28},{28,20},{20,12},{12,4},{4,0},{1,9},{9... | collective-permute-start | bytes 2359304 | tf_op jit(solution)/shard_map/ppermute | solution.py:403
  320.5 20.8 %collective-permute-start.7 = (bf16[192,2048]{1,0:T(8,128)(2,1)}, bf16[192,2048]{1,0:T(8,128)(2,1)}, u32[]{:S(2)}, u32[]{:S(2)}) collective-permute-start(bf16[192,2048]{1,0:T(8,128)(2,1)} %collective-permute-done.5.refs_5_), channel_id=1, source_target_pairs={{8,0},{16,8},{24,16},{28,24},{20,28},{12,20},{4,12},{0,4},{9,1},{1... | collective-permute-start | bytes 2359304 | tf_op jit(solution)/shard_map/ppermute | solution.py:403
  321.0 38.1 %collective-permute-start.2 = (bf16[256,2048]{1,0:T(8,128)(2,1)}, bf16[256,2048]{1,0:T(8,128)(2,1)}, u32[]{:S(2)}, u32[]{:S(2)}) collective-permute-start(bf16[256,2048]{1,0:T(8,128)(2,1)} %collective-permute-done.refs_0_), channel_id=1, source_target_pairs={{0,8},{8,16},{16,24},{24,28},{28,20},{20,12},{12,4},{4,0},{1,9},{9... | collective-permute-start | bytes 3145736 | tf_op jit(solution)/shard_map/ppermute | solution.py:402
  322.6 37.8 %collective-permute-start.3 = (bf16[256,2048]{1,0:T(8,128)(2,1)}, bf16[256,2048]{1,0:T(8,128)(2,1)}, u32[]{:S(2)}, u32[]{:S(2)}) collective-permute-start(bf16[256,2048]{1,0:T(8,128)(2,1)} %collective-permute-done.1.refs_1_), channel_id=1, source_target_pairs={{8,0},{16,8},{24,16},{28,24},{20,28},{12,20},{4,12},{0,4},{9,1},{1... | collective-permute-start | bytes 3145736 | tf_op jit(solution)/shard_map/ppermute | solution.py:402
  323.0 6.5 %copy-start.5 = (f32[384,1536]{0,1:T(8,128)S(1)}, f32[384,1536]{0,1:T(8,128)}, u32[]{:S(2)}) copy-start(f32[384,1536]{0,1:T(8,128)} %copy-done.4) | copy-start | bytes 7077892
  333.0 27.4 %copy-start = (bf16[512,2048]{1,0:T(8,128)(2,1)S(1)}, bf16[512,2048]{1,0:T(8,128)(2,1)}, u32[]{:S(2)}) copy-start(bf16[512,2048]{1,0:T(8,128)(2,1)} %w_ref.1) | copy-start | bytes 6291460
  360.4 1.4 copy-start.2
